TPU v7x, 32 devices: a whole 2x2x4 slice. The times are simulated.
32 devices in a mesh: rep: 2 (over x), seq: 16 (over z, y, core).
Axes of the slice: x: 2, y: 2, z: 4, core: 2. Of those that a mesh axis runs over, the one named last changes fastest.
Arguments:
- q_stream: bfloat16 [4096, 8192], P(('rep', 'seq')), parts along dimension 0, may hold values from -6 to 6
- k_stream: bfloat16 [4096, 8192], P(('rep', 'seq')), parts along dimension 0, may hold values from -6 to 6
- v_stream: bfloat16 [4096, 8192], P(('rep', 'seq')), parts along dimension 0, may hold values from -6 to 6
- feat_filter: float32 [3, 3, 8192], replicated, may hold values from -3.5 to 3.5
- long_filter: bfloat16 [512, 128], replicated, may hold values from -0.5 to 0.5
- skip_gain: float32 [8192], replicated, may hold values from -3 to 3
Outputs:
- mixed: bfloat16 [4096, 8192], P(('rep', 'seq')), parts along dimension 0
There are 2 independent parts, one for each index of `rep`. A program takes and returns all parts, laid end to end along the dimension named above; an argument that names none is the same for every part. Nothing has to cross between parts.
All inputs are finite; a program needn't handle non-finite values.
Results may differ from a plain program's by a relative error of at most 0.005.
Values may be sent and summed in bfloat16 or wider, within the bound.
A program may use at most 128 MiB of HBM per device.

v0:
```python
import jax
import jax.numpy as jnp
from jax import lax
from jax.sharding import PartitionSpec as P

GROUP_CH = 16
FILT = 128
FEAT = 3


def passed_along(shard, axis, by):
    length = lax.axis_size(axis)
    pairs = [(i, i + by) for i in range(length) if 0 <= i + by < length]
    return lax.ppermute(shard, axis, pairs)


def featurize(rim, local, taps):
    length = local.shape[0]
    extended = jnp.concatenate([rim, local], axis=0).astype(jnp.float32)
    total = taps[0] * extended[FEAT - 1 : FEAT - 1 + length]
    for j in range(1, FEAT):
        total = total + taps[j] * extended[FEAT - 1 - j : FEAT - 1 - j + length]
    return total


def causal_blocks(current, earlier, filters):
    length, width = current.shape
    count = length // FILT
    groups = filters.shape[0]
    blocks = current.reshape(count, FILT, groups, GROUP_CH)
    before = jnp.concatenate([earlier.reshape(1, FILT, groups, GROUP_CH), blocks[:-1]], axis=0)
    window = jnp.concatenate([before, blocks], axis=1)
    rows = lax.broadcasted_iota(jnp.int32, (FILT, 2 * FILT), 0)
    cols = lax.broadcasted_iota(jnp.int32, (FILT, 2 * FILT), 1)
    lags = FILT + rows - cols
    picks = jnp.arange(FILT, dtype=jnp.int32)
    onehot = (lags[None, :, :] == picks[:, None, None]).astype(jnp.bfloat16)
    toeplitz = jnp.einsum(
        "gk,kts->gts", filters, onehot, preferred_element_type=jnp.float32
    ).astype(jnp.bfloat16)
    result = jnp.einsum("gts,bsgc->btgc", toeplitz, window, preferred_element_type=jnp.float32)
    return result.reshape(length, width)


def shards(q_stream, k_stream, v_stream, feat_filter, long_filter, skip_gain):
    rows, width = q_stream.shape
    edge = FEAT - 1
    rims = passed_along(
        (q_stream[rows - edge :], k_stream[rows - edge :], v_stream[rows - edge :]), "seq", 1
    )
    q_feat = featurize(rims[0], q_stream, feat_filter[0])
    k_feat = featurize(rims[1], k_stream, feat_filter[1])
    v_feat = featurize(rims[2], v_stream, feat_filter[2])
    gated = (k_feat * v_feat).astype(jnp.bfloat16)
    trailing = passed_along(gated[rows - FILT + 1 :], "seq", 1)
    earlier = jnp.concatenate([jnp.zeros((1, width), jnp.bfloat16), trailing], axis=0)
    conv = causal_blocks(gated, earlier, long_filter)
    mixed = q_feat * (conv + skip_gain * gated.astype(jnp.float32))
    return mixed.astype(jnp.bfloat16)


def solution(mesh):
    in_specs = (
        P(("rep", "seq"), None),
        P(("rep", "seq"), None),
        P(("rep", "seq"), None),
        P(),
        P(),
        P(),
    )
    out_specs = P(("rep", "seq"), None)
    return jax.shard_map(shards, mesh=mesh, in_specs=in_specs, out_specs=out_specs, check_vma=False)
```

profile of v0, /device:TPU:0, one launch (start us, length us, event | category | flops | bytes accessed | tf_op | source)
XLA Modules:
  0.0 137.5 jit_solution(12762081072262178950)
XLA Ops:
  0.0 0.0 copy-start
  0.0 0.0 copy-start.2
  0.0 1.1 slice.88
  1.1 2.4 %collective-permute-start = (bf16[2,8192]{1,0:T(2,128)(2,1)S(1)}, bf16[2,8192]{1,0:T(2,128)(2,1)S(1)}, u32[]{:S(2)}, u32[]{:S(2)}) collective-permute-start(bf16[2,8192]{1,0:T(2,128)(2,1)S(1)} %slice.88), channel_id=1, source_target_pairs={{0,1},{1,2},{2,3},{3,4},{4,5},{5,6},{6,7},{7,8},{8,9},{9,10},{10,1... | collective-permute-start | bytes 98312 | tf_op jit(solution)/shard_map/ppermute | solution.py:14
  3.5 0.9 slice.102
  4.5 4.5 %collective-permute-start.2 = (bf16[2,8192]{1,0:T(2,128)(2,1)S(1)}, bf16[2,8192]{1,0:T(2,128)(2,1)S(1)}, u32[]{:S(2)}, u32[]{:S(2)}) collective-permute-start(bf16[2,8192]{1,0:T(2,128)(2,1)S(1)} %slice.102), channel_id=1, source_target_pairs={{0,1},{1,2},{2,3},{3,4},{4,5},{5,6},{6,7},{7,8},{8,9},{9,10},{10,1... | collective-permute-start | bytes 98312 | tf_op jit(solution)/shard_map/ppermute | solution.py:14
  9.0 0.9 slice.95
  9.9 1.9 %collective-permute-start.1 = (bf16[2,8192]{1,0:T(2,128)(2,1)S(1)}, bf16[2,8192]{1,0:T(2,128)(2,1)S(1)}, u32[]{:S(2)}, u32[]{:S(2)}) collective-permute-start(bf16[2,8192]{1,0:T(2,128)(2,1)S(1)} %slice.95), channel_id=1, source_target_pairs={{0,1},{1,2},{2,3},{3,4},{4,5},{5,6},{6,7},{7,8},{8,9},{9,10},{10,1... | collective-permute-start | bytes 98312 | tf_op jit(solution)/shard_map/ppermute | solution.py:14
  11.9 0.1 iota_subtract_fusion
  12.0 1.7 %fusion.19 = (f32[1,1,8192]{2,1,0:T(1,128)S(1)}, f32[1,1,8192]{2,1,0:T(1,128)S(1)}, f32[1,1,8192]{2,1,0:T(1,128)S(1)}, f32[1,1,8192]{2,1,0:T(1,128)S(1)}, f32[1,...) fusion(f32[3,3,8192]{2,1,0:T(4,128)} %param.9), kind=kLoop, calls=%fused_computation.35 | loop fusion | bytes 589824 | tf_op jit(solution)/shard_map/slice | solution.py:20
  13.7 4.4 %iota_compare_fusion = pred[128,128,256]{2,1,0:T(32,128)(4,1)} fusion(s32[128,256]{1,0:T(8,128)S(1)} %iota_subtract_fusion), kind=kLoop, calls=%fused_computation.3 | loop fusion | flops 4194304 | bytes 4325376 | tf_op jit(solution)/shard_map/eq | solution.py:37
  18.1 0.0 copy-start.3
  18.1 0.0 collective-permute-done.2
  18.1 0.0 copy-done.2
  18.1 0.6 maximum_convert_fusion.2
  18.7 0.0 collective-permute-done.1
  18.7 1.0 copy-done.3
  19.7 0.6 maximum_convert_fusion.1
  20.3 2.7 %fusion.7 = bf16[128,8192]{1,0:T(8,128)(2,1)S(1)} fusion(f32[130,8192]{1,0:T(8,128)S(1)} %maximum_convert_fusion.2, f32[130,8192]{1,0:T(8,128)S(1)} %maximum_convert_fusion.1, f32[8192]{0:T(1024)S(1)} %bitcast.35, f32[8192]{0:T(1024)S(1)} %bitcast.36, f32[8192]{0:T(1024)S(1)} %bitcast.31, f32[8192]{0:T(1024)S(1)} %bitcast.32, f32[8192]{0:T(1024)S(1)} %bitcast.33, ...), kind=kLoop, calls=%fused_computation.9 | loop fusion | flops 12582912 | bytes 27459584 | tf_op jit(solution)/shard_map/convert_element_type | solution.py:54
  23.0 1.9 %slice.118 = bf16[127,8192]{1,0:T(8,128)(2,1)} slice(bf16[128,8192]{1,0:T(8,128)(2,1)S(1)} %fusion.7), slice={[1:128], [0:8192]} | slice | bytes 4161536 | tf_op jit(solution)/shard_map/slice | solution.py:55
  24.9 4.8 %collective-permute-start.3 = (bf16[127,8192]{1,0:T(8,128)(2,1)}, bf16[127,8192]{1,0:T(8,128)(2,1)}, u32[]{:S(2)}, u32[]{:S(2)}) collective-permute-start(bf16[127,8192]{1,0:T(8,128)(2,1)} %slice.118), channel_id=1, source_target_pairs={{0,1},{1,2},{2,3},{3,4},{4,5},{5,6},{6,7},{7,8},{8,9},{9,10},{10,1... | collective-permute-start | bytes 6242312 | tf_op jit(solution)/shard_map/ppermute | solution.py:14
  29.7 0.0 copy-done
  29.7 16.1 %fusion.3 = bf16[128,256,512]{2,1,0:T(8,128)(2,1)} fusion(pred[128,128,256]{2,1,0:T(32,128)(4,1)} %iota_compare_fusion, bf16[512,128]{1,0:T(8,128)(2,1)S(1)} %copy-done), kind=kOutput, calls=%fused_computation.4 | convolution fusion | flops 4294967296 | bytes 37879808 | tf_op jit(solution)/shard_map/gk,kts->gts/dot_general | solution.py:38
  45.8 45.5 %copy.11 = bf16[128,256,512]{1,0,2:T(8,128)(2,1)} copy(bf16[128,256,512]{2,1,0:T(8,128)(2,1)} %fusion.3) | data formatting | bytes 67108864 | tf_op jit(solution)/shard_map/gk,kts->gts/dot_general | solution.py:38
  91.3 2.4 %copy.8 = bf16[128,8192]{0,1:T(8,128)(2,1)} copy(bf16[128,8192]{1,0:T(8,128)(2,1)S(1)} %fusion.7) | data formatting | bytes 4194304 | tf_op jit(solution)/shard_map/convert_element_type | solution.py:54
  93.7 0.0 collective-permute-done
  93.7 4.4 %maximum_convert_fusion = f32[130,8192]{1,0:T(8,128)} fusion(bf16[128,8192]{1,0:T(8,128)(2,1)} %param.6, bf16[2,8192]{1,0:T(2,128)(2,1)S(1)} %collective-permute-done), kind=kLoop, calls=%fused_computation.28 | loop fusion | flops 4259840 | bytes 6389760 | tf_op jit(solution)/shard_map/convert_element_type | solution.py:19
  98.1 0.0 collective-permute-done.3
  98.1 4.1 %copy.12 = bf16[127,8192]{0,1:T(8,128)(2,1)} copy(bf16[127,8192]{1,0:T(8,128)(2,1)} %collective-permute-done.3) | data formatting | bytes 4161536
  102.2 3.7 %concatenate.18.clone = bf16[128,8192]{0,1:T(8,128)(2,1)} pad(bf16[127,8192]{0,1:T(8,128)(2,1)} %copy.12, bf16[]{:T(256)} %constant.0.clone.1), padding=1_0x0_0 | pad | bytes 4177922 | tf_op jit(solution)/shard_map/concatenate | solution.py:56
  105.9 17.6 %fusion = f32[512,16,128]{2,1,0:T(8,128)} fusion(bf16[128,256,512]{1,0,2:T(8,128)(2,1)} %copy.11, bf16[1,128,512,16]{1,3,2,0:T(8,128)(2,1)} %bitcast.26, bf16[1,128,512,16]{1,3,2,0:T(8,128)(2,1)} %bitcast.27), kind=kOutput, calls=%fused_computation | convolution fusion | flops 545259520 | bytes 41943040 | tf_op jit(solution)/shard_map/gts,bsgc->btgc/dot_general | solution.py:41
  123.5 0.0 copy-start.4
  123.5 5.6 %copy.9 = f32[128,8192]{1,0:T(8,128)} copy(f32[128,8192]{0,1:T(8,128)} %bitcast.25) | data formatting | bytes 8388608 | tf_op jit(solution)/shard_map/reshape | solution.py:42
  129.1 0.0 copy-done.4
  129.1 0.0 copy-start.1
  129.1 8.4 %fusion.13 = bf16[128,8192]{1,0:T(8,128)(2,1)} fusion(f32[130,8192]{1,0:T(8,128)} %maximum_convert_fusion, f32[128,8192]{1,0:T(8,128)} %copy.9, bf16[128,8192]{1,0:T(8,128)(2,1)S(1)} %fusion.7, f32[8192]{0:T(1024)S(1)} %copy-done.4, f32[8192]{0:T(1024)S(1)} %bitcast.29, f32[8192]{0:T(1024)S(1)} %bitcast.30, f32[8192]{0:T(1024)S(1)} %bitcast.28), kind=kLoop, calls=%fused_computation.21 | loop fusion | flops 10485760 | bytes 21102592 | tf_op jit(solution)/shard_map/convert_element_type | solution.py:59
  137.5 0.0 copy-done.1
  (1 shorter events, 0.0 us)
Async XLA Ops:
  0.0 29.7 %copy-start = (bf16[512,128]{1,0:T(8,128)(2,1)S(1)}, bf16[512,128]{1,0:T(8,128)(2,1)}, u32[]{:S(2)}) copy-start(bf16[512,128]{1,0:T(8,128)(2,1)} %param.10) | copy-start | bytes 393220
  0.0 18.1 %copy-start.2 = (bf16[128,8192]{1,0:T(8,128)(2,1)S(1)}, bf16[128,8192]{1,0:T(8,128)(2,1)}, u32[]{:S(2)}) copy-start(bf16[128,8192]{1,0:T(8,128)(2,1)} %param.8) | copy-start | bytes 6291460
  1.1 92.6 %collective-permute-start = (bf16[2,8192]{1,0:T(2,128)(2,1)S(1)}, bf16[2,8192]{1,0:T(2,128)(2,1)S(1)}, u32[]{:S(2)}, u32[]{:S(2)}) collective-permute-start(bf16[2,8192]{1,0:T(2,128)(2,1)S(1)} %slice.88), channel_id=1, source_target_pairs={{0,1},{1,2},{2,3},{3,4},{4,5},{5,6},{6,7},{7,8},{8,9},{9,10},{10,1... | collective-permute-start | bytes 98312 | tf_op jit(solution)/shard_map/ppermute | solution.py:14
  4.5 13.7 %collective-permute-start.2 = (bf16[2,8192]{1,0:T(2,128)(2,1)S(1)}, bf16[2,8192]{1,0:T(2,128)(2,1)S(1)}, u32[]{:S(2)}, u32[]{:S(2)}) collective-permute-start(bf16[2,8192]{1,0:T(2,128)(2,1)S(1)} %slice.102), channel_id=1, source_target_pairs={{0,1},{1,2},{2,3},{3,4},{4,5},{5,6},{6,7},{7,8},{8,9},{9,10},{10,1... | collective-permute-start | bytes 98312 | tf_op jit(solution)/shard_map/ppermute | solution.py:14
  9.9 8.8 %collective-permute-start.1 = (bf16[2,8192]{1,0:T(2,128)(2,1)S(1)}, bf16[2,8192]{1,0:T(2,128)(2,1)S(1)}, u32[]{:S(2)}, u32[]{:S(2)}) collective-permute-start(bf16[2,8192]{1,0:T(2,128)(2,1)S(1)} %slice.95), channel_id=1, source_target_pairs={{0,1},{1,2},{2,3},{3,4},{4,5},{5,6},{6,7},{7,8},{8,9},{9,10},{10,1... | collective-permute-start | bytes 98312 | tf_op jit(solution)/shard_map/ppermute | solution.py:14
  18.1 1.6 %copy-start.3 = (bf16[128,8192]{1,0:T(8,128)(2,1)S(1)}, bf16[128,8192]{1,0:T(8,128)(2,1)}, u32[]{:S(2)}) copy-start(bf16[128,8192]{1,0:T(8,128)(2,1)} %param.7) | copy-start | bytes 6291460
  24.9 73.2 %collective-permute-start.3 = (bf16[127,8192]{1,0:T(8,128)(2,1)}, bf16[127,8192]{1,0:T(8,128)(2,1)}, u32[]{:S(2)}, u32[]{:S(2)}) collective-permute-start(bf16[127,8192]{1,0:T(8,128)(2,1)} %slice.118), channel_id=1, source_target_pairs={{0,1},{1,2},{2,3},{3,4},{4,5},{5,6},{6,7},{7,8},{8,9},{9,10},{10,1... | collective-permute-start | bytes 6242312 | tf_op jit(solution)/shard_map/ppermute | solution.py:14
  123.5 5.6 %copy-start.4 = (f32[8192]{0:T(1024)S(1)}, f32[8192]{0:T(1024)}, u32[]{:S(2)}) copy-start(f32[8192]{0:T(1024)} %param.11) | copy-start | bytes 98308
  129.1 8.4 %copy-start.1 = (bf16[512,128]{1,0:T(8,128)(2,1)S(1)}, bf16[512,128]{1,0:T(8,128)(2,1)}, u32[]{:S(2)}) copy-start(bf16[512,128]{1,0:T(8,128)(2,1)} %param.10) | copy-start | bytes 393220
where the time goes:
time: 139 us; the launch traced here: 138 us
  local copies, waits for them, and re-layouts  68.9 us (50%)
  matrix products  33.7 us (24%)
  other arithmetic  21.1 us (15%)
  starting transfers between devices  13.7 us (10%)
    dot_general x1, local copies, waits for them, and re-layouts, causal_blocks(): jnp.einsum('gk,kts->gts', filters, onehot, preferred_element_type=jnp.flo...  45.5 us
    dot_general x1, matrix products, causal_blocks(): jnp.einsum('gts,bsgc->btgc', toeplitz, window, preferred_element_type=jnp...  17.6 us
    dot_general x1, matrix products, causal_blocks(): jnp.einsum('gk,kts->gts', filters, onehot, preferred_element_type=jnp.flo...  16.1 us
    ppermute x4, starting transfers between devices, passed_along(): return lax.ppermute(shard, axis, pairs)  13.7 us
    convert_element_type x1, other arithmetic, shards(): return mixed.astype(jnp.bfloat16)  8.38 us
    reshape x1, local copies, waits for them, and re-layouts, causal_blocks(): return result.reshape(length, width)  5.63 us
    convert_element_type x3, other arithmetic, featurize(): extended = jnp.concatenate([rim, local], axis=0).astype(jnp.float32)  5.52 us
    unnamed x11, local copies, waits for them, and re-layouts  5.13 us
  transfers between devices with their start and end apart: 4, of which 0 were waited for; matrix products, arithmetic and copies ran while one was open for 60% of the time, Pallas kernels for 0%

commit v1 on v0

v1 whole, which is shorter than its diff:
```python
import functools

import jax
import jax.numpy as jnp
from jax import lax
from jax.experimental import pallas as pl
from jax.experimental.pallas import tpu as pltpu
from jax.sharding import PartitionSpec as P

GROUP_CH = 16
FILT = 128
FEAT = 3
LANES = 128
SUB = 16
CHUNK = 512
EARLY = 2
MESH = pl.DeviceIdType.MESH


def shifted(rim, x):
    ext = jnp.concatenate([rim, x], axis=0)
    return pltpu.roll(ext, 1, 0)[8:], pltpu.roll(ext, 2, 0)[8:]


def featurize(x, rim, taps):
    x = x.astype(jnp.float32)
    one, two = shifted(rim, x)
    return taps[0] * x + taps[1] * one + taps[2] * two


def kernel(
    n, q_hbm, k_hbm, v_hbm, feat_hbm, long_hbm, skip_hbm, out_hbm,
    q, k, v, feat, filt, skip, ends, rim_out, rim_in, gated, prev, mixed, toep,
    in_sem, end_sem, par_sem, send_sem, recv_sem, out_sem,
):
    chunks, rows, width = gated.shape
    tiles = width // LANES
    groups = filt.shape[0]
    me = lax.axis_index("seq")
    right, left = lax.rem(me + 1, n), lax.rem(me + n - 1, n)
    has_left, has_right = me > 0, me < n - 1

    barrier = pltpu.get_barrier_semaphore()

    @pl.when(has_left)
    def _():
        pl.semaphore_signal(barrier, inc=1, device_id={"seq": left}, device_id_type=MESH)

    streams = ((k_hbm, k), (v_hbm, v), (q_hbm, q))

    def end_copy(i):
        return pltpu.make_async_copy(
            streams[i][0].at[pl.ds(rows - 8, 8)], ends.at[i], end_sem.at[i])

    def in_copy(i, c):
        cols = pl.ds(pl.multiple_of(c * width, width), width)
        return pltpu.make_async_copy(
            streams[i][0].at[:, cols], streams[i][1].at[c], in_sem.at[i, c])

    params = ((feat_hbm, feat), (long_hbm, filt), (skip_hbm, skip))

    def par_copy(i):
        return pltpu.make_async_copy(params[i][0], params[i][1], par_sem.at[i])

    for i in range(3):
        end_copy(i).start()
    for c in range(EARLY):
        in_copy(0, c).start()
        in_copy(1, c).start()
        if c == 0:
            par_copy(0).start()

    @pl.loop(EARLY, chunks)
    def _(c):
        in_copy(0, c).start()
        in_copy(1, c).start()

    par_copy(1).start()
    par_copy(2).start()

    @pl.loop(0, chunks)
    def _(c):
        in_copy(2, c).start()

    def remote(src, dst, slot):
        return pltpu.make_async_remote_copy(
            src_ref=src, dst_ref=dst, send_sem=send_sem.at[slot],
            recv_sem=recv_sem.at[slot], device_id={"seq": right}, device_id_type=MESH)

    def rim_copy():
        return remote(rim_out, rim_in, chunks + EARLY)

    def whole_copy(c):
        return remote(gated.at[c], prev.at[c], c)

    def body_copy(c):
        part = pl.ds(16, rows - 16)
        return remote(gated.at[c, part], prev.at[c, part], c)

    def head_copy(c):
        part = pl.ds(0, 16)
        return remote(gated.at[c, part], prev.at[c, part], chunks + c)

    for i in range(3):
        end_copy(i).wait()
    row = lax.broadcasted_iota(jnp.int32, (8, LANES), 0)

    @pl.loop(0, chunks)
    def _(c):
        for t in range(tiles):
            cols = pl.ds(pl.multiple_of(c * width + t * LANES, LANES), LANES)
            last = [ends[i, :, cols].astype(jnp.float32) for i in range(3)]
            packed = jnp.where(
                row < 2, pltpu.roll(last[0], 2, 0),
                jnp.where(row < 4, pltpu.roll(last[1], 4, 0), pltpu.roll(last[2], 6, 0)))
            rim_out[:, cols] = packed.astype(jnp.bfloat16)

    @pl.when(has_right)
    def _():
        pl.semaphore_wait(barrier, 1)
        rim_copy().start()

    def taps_of(i, cols):
        return [feat[i, pl.ds(j, 1), cols] for j in range(FEAT)]

    def rim_of(i, cols):
        x = rim_in[:, cols].astype(jnp.float32)
        return pltpu.roll(x, 6 - 2 * i, 0)

    def columns(c, t):
        return pl.ds(pl.multiple_of(c * width + t * LANES, LANES), LANES)

    def gate(c, t, first, count, k_rim, v_rim):
        cols = columns(c, t)
        part, lanes = pl.ds(first, count), pl.ds(t * LANES, LANES)
        k_feat = featurize(k[c, part, lanes], k_rim, taps_of(1, cols))
        v_feat = featurize(v[c, part, lanes], v_rim, taps_of(2, cols))
        return (k_feat * v_feat).astype(jnp.bfloat16)

    zeros = jnp.zeros((8, LANES), jnp.float32)
    par_copy(0).wait()
    for c in range(EARLY):
        in_copy(0, c).wait()
        in_copy(1, c).wait()
        for t in range(tiles):
            lanes = pl.ds(t * LANES, LANES)
            gated[c, pl.ds(16, rows - 16), lanes] = gate(c, t, 0, rows, zeros, zeros)[16:]

        @pl.when(has_right)
        def _():
            body_copy(c).start()

    @pl.when(has_left)
    def _():
        rim_copy().wait_recv()

    @pl.when(jnp.logical_not(has_left))
    def _():
        rim_in[...] = jnp.zeros_like(rim_in)

        @pl.loop(0, chunks)
        def _(c):
            prev[c] = jnp.zeros((rows, width), jnp.bfloat16)

    for c in range(EARLY):
        for t in range(tiles):
            cols = columns(c, t)
            gated[c, pl.ds(0, 16), pl.ds(t * LANES, LANES)] = gate(
                c, t, 0, 16, rim_of(0, cols), rim_of(1, cols))

        @pl.when(has_right)
        def _():
            head_copy(c).start()

    @pl.loop(EARLY, chunks)
    def _(c):
        in_copy(0, c).wait()
        in_copy(1, c).wait()
        for t in range(tiles):
            cols = columns(c, t)
            gated[c, :, pl.ds(t * LANES, LANES)] = gate(
                c, t, 0, rows, rim_of(0, cols), rim_of(1, cols))

        @pl.when(has_right)
        def _():
            whole_copy(c).start()

    par_copy(1).wait()
    par_copy(2).wait()
    taps = lax.broadcasted_iota(jnp.int32, (FILT, 2 * LANES), 0)
    place = lax.broadcasted_iota(jnp.int32, (FILT, 2 * LANES), 1)
    total = taps + place
    for b in range(SUB):
        onehot = jnp.where(total == FILT + b, 1.0, 0.0).astype(jnp.bfloat16)
        moved = jnp.dot(filt[...], onehot, preferred_element_type=jnp.float32)
        for r in range(2):
            toep[r, pl.ds(b, groups, stride=SUB), :] = moved[:, r * LANES:(r + 1) * LANES]

    lane_group = lax.broadcasted_iota(jnp.int32, (SUB, LANES), 1) // GROUP_CH
    per_tile = LANES // GROUP_CH
    blocks = rows // SUB
    depth = FILT + SUB

    def mix(c):
        for t in range(tiles):
            cols, lanes = columns(c, t), pl.ds(t * LANES, LANES)
            first = pl.multiple_of((c * tiles + t) * LANES, LANES)
            own = gated[c, :, lanes]
            window = jnp.concatenate([prev[c, :, lanes], own], axis=0)
            left_part = toep[0, pl.ds(first, LANES), :].astype(jnp.bfloat16)
            right_part = toep[1, pl.ds(first, LANES), :].astype(jnp.bfloat16)
            lhs = jnp.concatenate([left_part, right_part[:, :depth - LANES]], axis=1)
            rhs = jnp.concatenate(
                [window[a * SUB:a * SUB + depth] for a in range(blocks)], axis=1)
            every = jnp.dot(lhs, rhs, preferred_element_type=jnp.float32)
            conv = []
            for a in range(blocks):
                mine = every[:SUB, a * LANES:(a + 1) * LANES]
                for g in range(1, per_tile):
                    mine = jnp.where(
                        lane_group == g,
                        every[g * SUB:(g + 1) * SUB, a * LANES:(a + 1) * LANES], mine)
                conv.append(mine)
            conv = jnp.concatenate(conv, axis=0)
            q_feat = featurize(q[c, :, lanes], rim_of(2, cols), taps_of(0, cols))
            direct = skip[:, cols] * own.astype(jnp.float32)
            mixed[c, :, lanes] = (q_feat * (conv + direct)).astype(jnp.bfloat16)

    def out_copy(c):
        cols = pl.ds(pl.multiple_of(c * width, width), width)
        return pltpu.make_async_copy(mixed.at[c], out_hbm.at[:, cols], out_sem.at[c])

    for c in range(EARLY):
        @pl.when(has_left)
        def _():
            body_copy(c).wait_recv()
            head_copy(c).wait_recv()

        in_copy(2, c).wait()
        mix(c)
        out_copy(c).start()

    @pl.loop(EARLY, chunks)
    def _(c):
        @pl.when(has_left)
        def _():
            whole_copy(c).wait_recv()

        in_copy(2, c).wait()
        mix(c)
        out_copy(c).start()

    @pl.when(has_right)
    def _():
        rim_copy().wait_send()
        for c in range(EARLY):
            body_copy(c).wait_send()
            head_copy(c).wait_send()

        @pl.loop(EARLY, chunks)
        def _(c):
            whole_copy(c).wait_send()

    @pl.loop(0, chunks)
    def _(c):
        out_copy(c).wait()


def shards(n, q_stream, k_stream, v_stream, feat_filter, long_filter, skip_gain):
    rows, channels = q_stream.shape
    groups = long_filter.shape[0]
    chunks = channels // CHUNK
    cut = pltpu.VMEM((chunks, rows, CHUNK), jnp.bfloat16)
    dma = pltpu.SemaphoreType.DMA
    return pl.pallas_call(
        functools.partial(kernel, n),
        out_shape=jax.ShapeDtypeStruct((rows, channels), jnp.bfloat16),
        in_specs=[pl.BlockSpec(memory_space=pl.ANY)] * 6,
        out_specs=pl.BlockSpec(memory_space=pl.ANY),
        scratch_shapes=[
            cut, cut, cut,
            pltpu.VMEM(feat_filter.shape, jnp.float32),
            pltpu.VMEM(long_filter.shape, jnp.bfloat16),
            pltpu.VMEM((1, channels), jnp.float32),
            pltpu.VMEM((3, 8, channels), jnp.bfloat16),
            pltpu.VMEM((8, channels), jnp.bfloat16),
            pltpu.VMEM((8, channels), jnp.bfloat16),
            cut, cut, cut,
            pltpu.VMEM((2, groups * SUB, LANES), jnp.float32),
            dma((3, chunks)), dma((3,)), dma((3,)),
            dma((chunks + EARLY + 1,)), dma((chunks + EARLY + 1,)), dma((chunks,)),
        ],
        compiler_params=pltpu.CompilerParams(collective_id=0, has_side_effects=True),
    )(q_stream, k_stream, v_stream, feat_filter, long_filter, skip_gain.reshape(1, channels))


def solution(mesh):
    n = mesh.shape["seq"]
    rows = P(("rep", "seq"), None)
    return jax.shard_map(
        functools.partial(shards, n), mesh=mesh,
        in_specs=(rows, rows, rows, P(), P(), P()), out_specs=rows, check_vma=False)
```

time: 139 us -> 33.1 us (0.24)
  the two profiles are of different devices: /device:TPU:0 before, /device:TPU:10 now
where the time goes in v1:
time: 33.1 us; the launch traced here: 32.9 us
  Pallas kernels  29.8 us (90%)
  local copies, waits for them, and re-layouts  3.1 us (9%)
    pallas_call x1, Pallas kernels, shards(): pl.pallas_call(functools.partial(kernel, n), out_shape=jax.ShapeDtypeStru...  29.8 us
    unnamed x1, local copies, waits for them, and re-layouts  3.1 us

profile of v1, /device:TPU:10, one launch (start us, length us, event | category | flops | bytes accessed | tf_op | source)
XLA Modules:
  0.0 32.9 jit_solution(5607492305065950559)
XLA Ops:
  0.0 29.8 %shard_map.64 = bf16[128,8192]{1,0:T(8,128)(2,1)} custom-call(bf16[128,8192]{1,0:T(8,128)(2,1)} %q_hbm.1, bf16[128,8192]{1,0:T(8,128)(2,1)} %k_hbm.1, bf16[128,8192]{1,0:T(8,128)(2,1)} %v_hbm.1, f32[3,3,8192]{2,1,0:T(4,128)} %feat_hbm.1, bf16[512,128]{1,0:T(8,128)(2,1)} %long_hbm.1, f32[1,8192]{1,0:T(1,128)} %bitcast.1), custom_call_target="tpu_custom_call" | custom-call | tf_op jit(solution)/shard_map/pallas_call | solution.py:275
  29.8 3.1 %copy.8 = bf16[128,8192]{1,0:T(8,128)(2,1)} copy(bf16[128,8192]{1,0:T(8,128)(2,1)} %shard_map.64) | data formatting | bytes 4194304

commit v2 on v1

--- a/solution.py
+++ b/solution.py
@@ -12,8 +12,9 @@
 FEAT = 3
 LANES = 128
 SUB = 16
-CHUNK = 512
-EARLY = 2
+CHUNK = 256
+EARLY = 4
+GRANT = 58 << 20
 MESH = pl.DeviceIdType.MESH
 
 
@@ -29,9 +30,9 @@
 
 
 def kernel(
-    n, q_hbm, k_hbm, v_hbm, feat_hbm, long_hbm, skip_hbm, out_hbm,
-    q, k, v, feat, filt, skip, ends, rim_out, rim_in, gated, prev, mixed, toep,
-    in_sem, end_sem, par_sem, send_sem, recv_sem, out_sem,
+    n, q_hbm, k_hbm, v_hbm, feat_hbm, long_hbm, skip_hbm, mixed,
+    q, k, v, feat, filt, skip, ends, rim_out, rim_in, gated, prev, toep,
+    in_sem, end_sem, par_sem, send_sem, recv_sem,
 ):
     chunks, rows, width = gated.shape
     tiles = width // LANES
@@ -226,10 +227,6 @@
             direct = skip[:, cols] * own.astype(jnp.float32)
             mixed[c, :, lanes] = (q_feat * (conv + direct)).astype(jnp.bfloat16)
 
-    def out_copy(c):
-        cols = pl.ds(pl.multiple_of(c * width, width), width)
-        return pltpu.make_async_copy(mixed.at[c], out_hbm.at[:, cols], out_sem.at[c])
-
     for c in range(EARLY):
         @pl.when(has_left)
         def _():
@@ -238,7 +235,6 @@
 
         in_copy(2, c).wait()
         mix(c)
-        out_copy(c).start()
 
     @pl.loop(EARLY, chunks)
     def _(c):
@@ -248,7 +244,6 @@
 
         in_copy(2, c).wait()
         mix(c)
-        out_copy(c).start()
 
     @pl.when(has_right)
     def _():
@@ -261,9 +256,18 @@
         def _(c):
             whole_copy(c).wait_send()
 
-    @pl.loop(0, chunks)
-    def _(c):
-        out_copy(c).wait()
+
+def drain(mixed, out_hbm, sem):
+    chunks, _, width = mixed.shape
+
+    def copy(c):
+        return pltpu.make_async_copy(
+            mixed.at[c], out_hbm.at[:, c * width:(c + 1) * width], sem.at[c])
+
+    for c in range(chunks):
+        copy(c).start()
+    for c in range(chunks):
+        copy(c).wait()
 
 
 def shards(n, q_stream, k_stream, v_stream, feat_filter, long_filter, skip_gain):
@@ -272,11 +276,11 @@
     chunks = channels // CHUNK
     cut = pltpu.VMEM((chunks, rows, CHUNK), jnp.bfloat16)
     dma = pltpu.SemaphoreType.DMA
-    return pl.pallas_call(
+    mixed = pl.pallas_call(
         functools.partial(kernel, n),
-        out_shape=jax.ShapeDtypeStruct((rows, channels), jnp.bfloat16),
-        in_specs=[pl.BlockSpec(memory_space=pl.ANY)] * 6,
-        out_specs=pl.BlockSpec(memory_space=pl.ANY),
+        out_shape=cut,
+        in_specs=[pl.BlockSpec(memory_space=pltpu.HBM)] * 6,
+        out_specs=pl.BlockSpec(memory_space=pltpu.VMEM),
         scratch_shapes=[
             cut, cut, cut,
             pltpu.VMEM(feat_filter.shape, jnp.float32),
@@ -285,13 +289,22 @@
             pltpu.VMEM((3, 8, channels), jnp.bfloat16),
             pltpu.VMEM((8, channels), jnp.bfloat16),
             pltpu.VMEM((8, channels), jnp.bfloat16),
-            cut, cut, cut,
+            cut, cut,
             pltpu.VMEM((2, groups * SUB, LANES), jnp.float32),
             dma((3, chunks)), dma((3,)), dma((3,)),
-            dma((chunks + EARLY + 1,)), dma((chunks + EARLY + 1,)), dma((chunks,)),
+            dma((chunks + EARLY + 1,)), dma((chunks + EARLY + 1,)),
         ],
-        compiler_params=pltpu.CompilerParams(collective_id=0, has_side_effects=True),
+        compiler_params=pltpu.CompilerParams(
+            collective_id=0, has_side_effects=True, vmem_limit_bytes=GRANT),
     )(q_stream, k_stream, v_stream, feat_filter, long_filter, skip_gain.reshape(1, channels))
+    return pl.pallas_call(
+        drain,
+        out_shape=jax.ShapeDtypeStruct((rows, channels), jnp.bfloat16),
+        in_specs=[pl.BlockSpec(memory_space=pltpu.VMEM)],
+        out_specs=pl.BlockSpec(memory_space=pl.ANY),
+        scratch_shapes=[dma((chunks,))],
+        compiler_params=pltpu.CompilerParams(vmem_limit_bytes=8 << 20),
+    )(mixed)
 
 
 def solution(mesh):

time: 33.1 us -> 31.5 us (0.952)
  local copies, waits for them, and re-layouts: 3.1 us -> 0 us
  Pallas kernels: 29.8 us -> 31.4 us
    unnamed x1 -> x0, local copies, waits for them, and re-layouts: 3.1 us -> none
    pallas_call x1 -> x2, Pallas kernels: 29.8 us -> 31.4 us  [the longest x1 29.8 us: shards(): pl.pallas_call(functools.partial(kernel, n), out_shape=cut, in_specs=[pl....]
where the time goes in v2:
time: 31.5 us; the launch traced here: 31.4 us
  Pallas kernels  31.4 us (100%)
    pallas_call x1, Pallas kernels, shards(): pl.pallas_call(functools.partial(kernel, n), out_shape=cut, in_specs=[pl....  29.8 us
    pallas_call x1, Pallas kernels, shards(): pl.pallas_call(drain, out_shape=jax.ShapeDtypeStruct((rows, channels), jn...  1.57 us

profile of v2, /device:TPU:10, one launch (start us, length us, event | category | flops | bytes accessed | tf_op | source)
XLA Modules:
  0.0 31.4 jit_solution(4377263888236978739)
XLA Ops:
  0.0 29.8 %shard_map.64.mixed = bf16[32,128,256]{2,1,0:T(8,128)(2,1)S(1)} custom-call(bf16[128,8192]{1,0:T(8,128)(2,1)} %q_hbm.1, bf16[128,8192]{1,0:T(8,128)(2,1)} %k_hbm.1, bf16[128,8192]{1,0:T(8,128)(2,1)} %v_hbm.1, f32[3,3,8192]{2,1,0:T(4,128)} %feat_hbm.1, bf16[512,128]{1,0:T(8,128)(2,1)} %long_hbm.1, f32[1,8192]{1,0:T(1,128)} %bitcast.1), custom_call_target="tpu_custom_call" | custom-call | tf_op jit(solution)/shard_map/pallas_call | solution.py:279
  29.8 1.6 %shard_map.65 = bf16[128,8192]{1,0:T(8,128)(2,1)} custom-call(bf16[32,128,256]{2,1,0:T(8,128)(2,1)S(1)} %shard_map.64.mixed), custom_call_target="tpu_custom_call" | custom-call | tf_op jit(solution)/shard_map/pallas_call | solution.py:300

commit v3 on v2

--- a/solution.py
+++ b/solution.py
@@ -12,7 +12,7 @@
 FEAT = 3
 LANES = 128
 SUB = 16
-CHUNK = 256
+CHUNK = 512
 EARLY = 4
 GRANT = 58 << 20
 MESH = pl.DeviceIdType.MESH
@@ -31,7 +31,7 @@
 
 def kernel(
     n, q_hbm, k_hbm, v_hbm, feat_hbm, long_hbm, skip_hbm, mixed,
-    q, k, v, feat, filt, skip, ends, rim_out, rim_in, gated, prev, toep,
+    q, k, v, feat, filt, skip, ends, kv_out, kv_in, q_out, q_in, gated, prev, toep,
     in_sem, end_sem, par_sem, send_sem, recv_sem,
 ):
     chunks, rows, width = gated.shape
@@ -63,33 +63,25 @@
     def par_copy(i):
         return pltpu.make_async_copy(params[i][0], params[i][1], par_sem.at[i])
 
+    in_copy(0, 0).start()
+    in_copy(1, 0).start()
+    par_copy(0).start()
     for i in range(3):
         end_copy(i).start()
-    for c in range(EARLY):
+    for c in range(1, EARLY):
         in_copy(0, c).start()
         in_copy(1, c).start()
-        if c == 0:
-            par_copy(0).start()
-
-    @pl.loop(EARLY, chunks)
-    def _(c):
-        in_copy(0, c).start()
-        in_copy(1, c).start()
-
-    par_copy(1).start()
-    par_copy(2).start()
-
-    @pl.loop(0, chunks)
-    def _(c):
-        in_copy(2, c).start()
 
     def remote(src, dst, slot):
         return pltpu.make_async_remote_copy(
             src_ref=src, dst_ref=dst, send_sem=send_sem.at[slot],
             recv_sem=recv_sem.at[slot], device_id={"seq": right}, device_id_type=MESH)
 
-    def rim_copy():
-        return remote(rim_out, rim_in, chunks + EARLY)
+    def kv_copy():
+        return remote(kv_out, kv_in, chunks + EARLY)
+
+    def q_copy():
+        return remote(q_out, q_in, chunks + EARLY + 1)
 
     def whole_copy(c):
         return remote(gated.at[c], prev.at[c], c)
@@ -102,31 +94,61 @@
         part = pl.ds(0, 16)
         return remote(gated.at[c, part], prev.at[c, part], chunks + c)
 
-    for i in range(3):
-        end_copy(i).wait()
     row = lax.broadcasted_iota(jnp.int32, (8, LANES), 0)
 
-    @pl.loop(0, chunks)
-    def _(c):
-        for t in range(tiles):
-            cols = pl.ds(pl.multiple_of(c * width + t * LANES, LANES), LANES)
-            last = [ends[i, :, cols].astype(jnp.float32) for i in range(3)]
-            packed = jnp.where(
-                row < 2, pltpu.roll(last[0], 2, 0),
-                jnp.where(row < 4, pltpu.roll(last[1], 4, 0), pltpu.roll(last[2], 6, 0)))
-            rim_out[:, cols] = packed.astype(jnp.bfloat16)
-
-    @pl.when(has_right)
-    def _():
-        pl.semaphore_wait(barrier, 1)
-        rim_copy().start()
+    def last_rows(i, at):
+        return ends[i, :, pl.ds(pl.multiple_of(at, LANES), LANES)].astype(jnp.float32)
+
+    def pack_kv():
+        half = kv_out.shape[1]
+
+        @pl.loop(0, half // width)
+        def _(c):
+            for t in range(tiles):
+                at = c * width + t * LANES
+                packed = jnp.where(
+                    row < 2, pltpu.roll(last_rows(0, at), 2, 0),
+                    jnp.where(
+                        row < 4, pltpu.roll(last_rows(1, at), 4, 0),
+                        jnp.where(
+                            row < 6, pltpu.roll(last_rows(0, at + half), 6, 0),
+                            last_rows(1, at + half))))
+                kv_out[:, pl.ds(pl.multiple_of(at, LANES), LANES)] = packed.astype(jnp.bfloat16)
+
+    def pack_q():
+        fourth = q_out.shape[1]
+
+        @pl.loop(0, fourth // width)
+        def _(c):
+            for t in range(tiles):
+                at = c * width + t * LANES
+                packed = last_rows(2, at + 3 * fourth)
+                for m in range(3):
+                    packed = jnp.where(
+                        row // 2 == m, pltpu.roll(last_rows(2, at + m * fourth), 2 + 2 * m, 0),
+                        packed)
+                q_out[:, pl.ds(pl.multiple_of(at, LANES), LANES)] = packed.astype(jnp.bfloat16)
 
     def taps_of(i, cols):
         return [feat[i, pl.ds(j, 1), cols] for j in range(FEAT)]
 
-    def rim_of(i, cols):
-        x = rim_in[:, cols].astype(jnp.float32)
-        return pltpu.roll(x, 6 - 2 * i, 0)
+    def kv_rims(c, t):
+        per_half = chunks // 2
+        upper = c >= per_half
+        at = lax.rem(c, per_half) * width + t * LANES
+        x = kv_in[:, pl.ds(pl.multiple_of(at, LANES), LANES)].astype(jnp.float32)
+        return (jnp.where(upper, pltpu.roll(x, 2, 0), pltpu.roll(x, 6, 0)),
+                jnp.where(upper, x, pltpu.roll(x, 4, 0)))
+
+    def q_rim(c, t):
+        per_fourth = chunks // 4
+        m = c // per_fourth
+        at = lax.rem(c, per_fourth) * width + t * LANES
+        x = q_in[:, pl.ds(pl.multiple_of(at, LANES), LANES)].astype(jnp.float32)
+        rim = x
+        for i in range(3):
+            rim = jnp.where(m == i, pltpu.roll(x, 6 - 2 * i, 0), rim)
+        return rim
 
     def columns(c, t):
         return pl.ds(pl.multiple_of(c * width + t * LANES, LANES), LANES)
@@ -147,17 +169,37 @@
             lanes = pl.ds(t * LANES, LANES)
             gated[c, pl.ds(16, rows - 16), lanes] = gate(c, t, 0, rows, zeros, zeros)[16:]
 
-        @pl.when(has_right)
-        def _():
-            body_copy(c).start()
+        if c == 0:
+            @pl.when(has_right)
+            def _():
+                pl.semaphore_wait(barrier, 1)
+                body_copy(0).start()
+
+            end_copy(0).wait()
+            end_copy(1).wait()
+            pack_kv()
+
+            @pl.when(has_right)
+            def _():
+                kv_copy().start()
+        else:
+            @pl.when(has_right)
+            def _():
+                body_copy(c).start()
+
+    @pl.loop(EARLY, chunks)
+    def _(c):
+        in_copy(0, c).start()
+        in_copy(1, c).start()
 
     @pl.when(has_left)
     def _():
-        rim_copy().wait_recv()
+        kv_copy().wait_recv()
 
     @pl.when(jnp.logical_not(has_left))
     def _():
-        rim_in[...] = jnp.zeros_like(rim_in)
+        kv_in[...] = jnp.zeros_like(kv_in)
+        q_in[...] = jnp.zeros_like(q_in)
 
         @pl.loop(0, chunks)
         def _(c):
@@ -165,22 +207,33 @@
 
     for c in range(EARLY):
         for t in range(tiles):
-            cols = columns(c, t)
             gated[c, pl.ds(0, 16), pl.ds(t * LANES, LANES)] = gate(
-                c, t, 0, 16, rim_of(0, cols), rim_of(1, cols))
+                c, t, 0, 16, *kv_rims(c, t))
 
         @pl.when(has_right)
         def _():
             head_copy(c).start()
+
+    end_copy(2).wait()
+    pack_q()
+
+    @pl.when(has_right)
+    def _():
+        q_copy().start()
+
+    par_copy(1).start()
+    par_copy(2).start()
+
+    @pl.loop(0, chunks)
+    def _(c):
+        in_copy(2, c).start()
 
     @pl.loop(EARLY, chunks)
     def _(c):
         in_copy(0, c).wait()
         in_copy(1, c).wait()
         for t in range(tiles):
-            cols = columns(c, t)
-            gated[c, :, pl.ds(t * LANES, LANES)] = gate(
-                c, t, 0, rows, rim_of(0, cols), rim_of(1, cols))
+            gated[c, :, pl.ds(t * LANES, LANES)] = gate(c, t, 0, rows, *kv_rims(c, t))
 
         @pl.when(has_right)
         def _():
@@ -223,9 +276,13 @@
                         every[g * SUB:(g + 1) * SUB, a * LANES:(a + 1) * LANES], mine)
                 conv.append(mine)
             conv = jnp.concatenate(conv, axis=0)
-            q_feat = featurize(q[c, :, lanes], rim_of(2, cols), taps_of(0, cols))
+            q_feat = featurize(q[c, :, lanes], q_rim(c, t), taps_of(0, cols))
             direct = skip[:, cols] * own.astype(jnp.float32)
             mixed[c, :, lanes] = (q_feat * (conv + direct)).astype(jnp.bfloat16)
+
+    @pl.when(has_left)
+    def _():
+        q_copy().wait_recv()
 
     for c in range(EARLY):
         @pl.when(has_left)
@@ -247,7 +304,8 @@
 
     @pl.when(has_right)
     def _():
-        rim_copy().wait_send()
+        kv_copy().wait_send()
+        q_copy().wait_send()
         for c in range(EARLY):
             body_copy(c).wait_send()
             head_copy(c).wait_send()
@@ -287,12 +345,14 @@
             pltpu.VMEM(long_filter.shape, jnp.bfloat16),
             pltpu.VMEM((1, channels), jnp.float32),
             pltpu.VMEM((3, 8, channels), jnp.bfloat16),
-            pltpu.VMEM((8, channels), jnp.bfloat16),
-            pltpu.VMEM((8, channels), jnp.bfloat16),
+            pltpu.VMEM((8, channels // 2), jnp.bfloat16),
+            pltpu.VMEM((8, channels // 2), jnp.bfloat16),
+            pltpu.VMEM((8, channels // 4), jnp.bfloat16),
+            pltpu.VMEM((8, channels // 4), jnp.bfloat16),
             cut, cut,
             pltpu.VMEM((2, groups * SUB, LANES), jnp.float32),
             dma((3, chunks)), dma((3,)), dma((3,)),
-            dma((chunks + EARLY + 1,)), dma((chunks + EARLY + 1,)),
+            dma((chunks + EARLY + 2,)), dma((chunks + EARLY + 2,)),
         ],
         compiler_params=pltpu.CompilerParams(
             collective_id=0, has_side_effects=True, vmem_limit_bytes=GRANT),

time: 31.5 us -> 30.4 us (0.965)
  Pallas kernels: 31.4 us -> 30.2 us
    pallas_call x1, Pallas kernels: 29.8 us -> 28.8 us  [shards(): pl.pallas_call(functools.partial(kernel, n), out_shape=cut, in_specs=[pl....]
where the time goes in v3:
time: 30.4 us; the launch traced here: 30.3 us
  Pallas kernels  30.2 us (99%)
    pallas_call x1, Pallas kernels, shards(): pl.pallas_call(functools.partial(kernel, n), out_shape=cut, in_specs=[pl....  28.8 us
    pallas_call x1, Pallas kernels, shards(): pl.pallas_call(drain, out_shape=jax.ShapeDtypeStruct((rows, channels), jn...  1.44 us

profile of v3, /device:TPU:10, one launch (start us, length us, event | category | flops | bytes accessed | tf_op | source)
XLA Modules:
  0.0 30.3 jit_solution(10349228183533775776)
XLA Ops:
  0.0 28.8 %shard_map.64.mixed = bf16[16,128,512]{2,1,0:T(8,128)(2,1)S(1)} custom-call(bf16[128,8192]{1,0:T(8,128)(2,1)} %q_hbm.1, bf16[128,8192]{1,0:T(8,128)(2,1)} %k_hbm.1, bf16[128,8192]{1,0:T(8,128)(2,1)} %v_hbm.1, f32[3,3,8192]{2,1,0:T(4,128)} %feat_hbm.1, bf16[512,128]{1,0:T(8,128)(2,1)} %long_hbm.1, f32[1,8192]{1,0:T(1,128)} %bitcast.1), custom_call_target="tpu_custom_call" | custom-call | tf_op jit(solution)/shard_map/pallas_call | solution.py:337
  28.8 1.4 %shard_map.65 = bf16[128,8192]{1,0:T(8,128)(2,1)} custom-call(bf16[16,128,512]{2,1,0:T(8,128)(2,1)S(1)} %shard_map.64.mixed), custom_call_target="tpu_custom_call" | custom-call | tf_op jit(solution)/shard_map/pallas_call | solution.py:360

commit v4 on v3

--- a/solution.py
+++ b/solution.py
@@ -89,6 +89,17 @@
     def body_copy(c):
         part = pl.ds(16, rows - 16)
         return remote(gated.at[c, part], prev.at[c, part], c)
+
+    last = chunks - 1
+    spare = chunks + EARLY + 2
+
+    def first_copy(h):
+        part, lanes = pl.ds(16, rows - 16), pl.ds(h * (width // 2), width // 2)
+        return remote(gated.at[0, part, lanes], prev.at[0, part, lanes], spare + h)
+
+    def last_copy(t):
+        lanes = pl.ds(t * LANES, LANES)
+        return remote(gated.at[last, :, lanes], prev.at[last, :, lanes], spare + 2 + t)
 
     def head_copy(c):
         part = pl.ds(0, 16)
@@ -168,12 +179,16 @@
         for t in range(tiles):
             lanes = pl.ds(t * LANES, LANES)
             gated[c, pl.ds(16, rows - 16), lanes] = gate(c, t, 0, rows, zeros, zeros)[16:]
+            if c == 0 and t == tiles // 2 - 1:
+                @pl.when(has_right)
+                def _():
+                    pl.semaphore_wait(barrier, 1)
+                    first_copy(0).start()
 
         if c == 0:
             @pl.when(has_right)
             def _():
-                pl.semaphore_wait(barrier, 1)
-                body_copy(0).start()
+                first_copy(1).start()
 
             end_copy(0).wait()
             end_copy(1).wait()
@@ -235,9 +250,14 @@
         for t in range(tiles):
             gated[c, :, pl.ds(t * LANES, LANES)] = gate(c, t, 0, rows, *kv_rims(c, t))
 
-        @pl.when(has_right)
+        @pl.when(jnp.logical_and(has_right, c < last))
         def _():
             whole_copy(c).start()
+
+    @pl.when(has_right)
+    def _():
+        for t in range(tiles):
+            last_copy(t).start()
 
     par_copy(1).wait()
     par_copy(2).wait()
@@ -255,8 +275,8 @@
     blocks = rows // SUB
     depth = FILT + SUB
 
-    def mix(c):
-        for t in range(tiles):
+    def mix(c, only=None):
+        for t in range(tiles) if only is None else (only,):
             cols, lanes = columns(c, t), pl.ds(t * LANES, LANES)
             first = pl.multiple_of((c * tiles + t) * LANES, LANES)
             own = gated[c, :, lanes]
@@ -287,13 +307,17 @@
     for c in range(EARLY):
         @pl.when(has_left)
         def _():
-            body_copy(c).wait_recv()
+            if c == 0:
+                first_copy(0).wait_recv()
+                first_copy(1).wait_recv()
+            else:
+                body_copy(c).wait_recv()
             head_copy(c).wait_recv()
 
         in_copy(2, c).wait()
         mix(c)
 
-    @pl.loop(EARLY, chunks)
+    @pl.loop(EARLY, last)
     def _(c):
         @pl.when(has_left)
         def _():
@@ -302,17 +326,31 @@
         in_copy(2, c).wait()
         mix(c)
 
+    in_copy(2, last).wait()
+    for t in range(tiles):
+        @pl.when(has_left)
+        def _():
+            last_copy(t).wait_recv()
+
+        mix(last, t)
+
     @pl.when(has_right)
     def _():
         kv_copy().wait_send()
         q_copy().wait_send()
-        for c in range(EARLY):
+        first_copy(0).wait_send()
+        first_copy(1).wait_send()
+        head_copy(0).wait_send()
+        for c in range(1, EARLY):
             body_copy(c).wait_send()
             head_copy(c).wait_send()
 
-        @pl.loop(EARLY, chunks)
+        @pl.loop(EARLY, last)
         def _(c):
             whole_copy(c).wait_send()
+
+        for t in range(tiles):
+            last_copy(t).wait_send()
 
 
 def drain(mixed, out_hbm, sem):
@@ -334,6 +372,7 @@
     chunks = channels // CHUNK
     cut = pltpu.VMEM((chunks, rows, CHUNK), jnp.bfloat16)
     dma = pltpu.SemaphoreType.DMA
+    remotes = chunks + EARLY + 4 + CHUNK // LANES
     mixed = pl.pallas_call(
         functools.partial(kernel, n),
         out_shape=cut,
@@ -352,7 +391,7 @@
             cut, cut,
             pltpu.VMEM((2, groups * SUB, LANES), jnp.float32),
             dma((3, chunks)), dma((3,)), dma((3,)),
-            dma((chunks + EARLY + 2,)), dma((chunks + EARLY + 2,)),
+            dma((remotes,)), dma((remotes,)),
         ],
         compiler_params=pltpu.CompilerParams(
             collective_id=0, has_side_effects=True, vmem_limit_bytes=GRANT),

time: 30.4 us -> 30.3 us (level)
  no operation moved by 1% of the time
where the time goes in v4:
time: 30.3 us; the launch traced here: 30.2 us
  Pallas kernels  30.1 us (99%)
    pallas_call x1, Pallas kernels, shards(): pl.pallas_call(functools.partial(kernel, n), out_shape=cut, in_specs=[pl....  28.7 us
    pallas_call x1, Pallas kernels, shards(): pl.pallas_call(drain, out_shape=jax.ShapeDtypeStruct((rows, channels), jn...  1.44 us

profile of v4, /device:TPU:10, one launch (start us, length us, event | category | flops | bytes accessed | tf_op | source)
XLA Modules:
  0.0 30.2 jit_solution(10647479036921202850)
XLA Ops:
  0.0 28.7 %shard_map.64.mixed = bf16[16,128,512]{2,1,0:T(8,128)(2,1)S(1)} custom-call(bf16[128,8192]{1,0:T(8,128)(2,1)} %q_hbm.1, bf16[128,8192]{1,0:T(8,128)(2,1)} %k_hbm.1, bf16[128,8192]{1,0:T(8,128)(2,1)} %v_hbm.1, f32[3,3,8192]{2,1,0:T(4,128)} %feat_hbm.1, bf16[512,128]{1,0:T(8,128)(2,1)} %long_hbm.1, f32[1,8192]{1,0:T(1,128)} %bitcast.1), custom_call_target="tpu_custom_call" | custom-call | tf_op jit(solution)/shard_map/pallas_call | solution.py:376
  28.7 1.4 %shard_map.65 = bf16[128,8192]{1,0:T(8,128)(2,1)} custom-call(bf16[16,128,512]{2,1,0:T(8,128)(2,1)S(1)} %shard_map.64.mixed), custom_call_target="tpu_custom_call" | custom-call | tf_op jit(solution)/shard_map/pallas_call | solution.py:399

commit v5 on v3

--- a/solution.py
+++ b/solution.py
@@ -63,11 +63,19 @@
     def par_copy(i):
         return pltpu.make_async_copy(params[i][0], params[i][1], par_sem.at[i])
 
+    def feat_copy(first, count):
+        cols = pl.ds(first, count)
+        return pltpu.make_async_copy(
+            feat_hbm.at[:, :, cols], feat.at[:, :, cols],
+            par_sem.at[0] if first == 0 else par_sem.at[3])
+
     in_copy(0, 0).start()
     in_copy(1, 0).start()
-    par_copy(0).start()
-    for i in range(3):
+    feat_copy(0, width).start()
+    for i in range(2):
         end_copy(i).start()
+    feat_copy(width, chunks * width - width).start()
+    end_copy(2).start()
     for c in range(1, EARLY):
         in_copy(0, c).start()
         in_copy(1, c).start()
@@ -161,8 +169,10 @@
         return (k_feat * v_feat).astype(jnp.bfloat16)
 
     zeros = jnp.zeros((8, LANES), jnp.float32)
-    par_copy(0).wait()
+    feat_copy(0, width).wait()
     for c in range(EARLY):
+        if c == 1:
+            feat_copy(width, chunks * width - width).wait()
         in_copy(0, c).wait()
         in_copy(1, c).wait()
         for t in range(tiles):
@@ -278,7 +288,7 @@
             conv = jnp.concatenate(conv, axis=0)
             q_feat = featurize(q[c, :, lanes], q_rim(c, t), taps_of(0, cols))
             direct = skip[:, cols] * own.astype(jnp.float32)
-            mixed[c, :, lanes] = (q_feat * (conv + direct)).astype(jnp.bfloat16)
+            mixed[:, cols] = (q_feat * (conv + direct)).astype(jnp.bfloat16)
 
     @pl.when(has_left)
     def _():
@@ -316,16 +326,17 @@
 
 
 def drain(mixed, out_hbm, sem):
-    chunks, _, width = mixed.shape
-
-    def copy(c):
-        return pltpu.make_async_copy(
-            mixed.at[c], out_hbm.at[:, c * width:(c + 1) * width], sem.at[c])
-
-    for c in range(chunks):
-        copy(c).start()
-    for c in range(chunks):
-        copy(c).wait()
+    blocks = sem.shape[0]
+    height = mixed.shape[0] // blocks
+
+    def copy(b):
+        part = pl.ds(b * height, height)
+        return pltpu.make_async_copy(mixed.at[part], out_hbm.at[part], sem.at[b])
+
+    for b in range(blocks):
+        copy(b).start()
+    for b in range(blocks):
+        copy(b).wait()
 
 
 def shards(n, q_stream, k_stream, v_stream, feat_filter, long_filter, skip_gain):
@@ -336,7 +347,7 @@
     dma = pltpu.SemaphoreType.DMA
     mixed = pl.pallas_call(
         functools.partial(kernel, n),
-        out_shape=cut,
+        out_shape=pltpu.VMEM((rows, channels), jnp.bfloat16),
         in_specs=[pl.BlockSpec(memory_space=pltpu.HBM)] * 6,
         out_specs=pl.BlockSpec(memory_space=pltpu.VMEM),
         scratch_shapes=[
@@ -351,7 +362,7 @@
             pltpu.VMEM((8, channels // 4), jnp.bfloat16),
             cut, cut,
             pltpu.VMEM((2, groups * SUB, LANES), jnp.float32),
-            dma((3, chunks)), dma((3,)), dma((3,)),
+            dma((3, chunks)), dma((3,)), dma((4,)),
             dma((chunks + EARLY + 2,)), dma((chunks + EARLY + 2,)),
         ],
         compiler_params=pltpu.CompilerParams(
@@ -362,7 +373,7 @@
         out_shape=jax.ShapeDtypeStruct((rows, channels), jnp.bfloat16),
         in_specs=[pl.BlockSpec(memory_space=pltpu.VMEM)],
         out_specs=pl.BlockSpec(memory_space=pl.ANY),
-        scratch_shapes=[dma((chunks,))],
+        scratch_shapes=[dma((rows // 16,))],
         compiler_params=pltpu.CompilerParams(vmem_limit_bytes=8 << 20),
     )(mixed)
 

time: 30.4 us -> 30.3 us (level)
  no operation moved by 1% of the time
where the time goes in v5:
time: 30.3 us; the launch traced here: 30.2 us
  Pallas kernels  30.2 us (100%)
    pallas_call x1, Pallas kernels, shards(): pl.pallas_call(functools.partial(kernel, n), out_shape=pltpu.VMEM((rows,...  28.8 us
    pallas_call x1, Pallas kernels, shards(): pl.pallas_call(drain, out_shape=jax.ShapeDtypeStruct((rows, channels), jn...  1.38 us

profile of v5, /device:TPU:10, one launch (start us, length us, event | category | flops | bytes accessed | tf_op | source)
XLA Modules:
  0.0 30.2 jit_solution(14798878784024392729)
XLA Ops:
  0.0 28.8 %shard_map.64.mixed = bf16[128,8192]{1,0:T(8,128)(2,1)S(1)} custom-call(bf16[128,8192]{1,0:T(8,128)(2,1)} %q_hbm.1, bf16[128,8192]{1,0:T(8,128)(2,1)} %k_hbm.1, bf16[128,8192]{1,0:T(8,128)(2,1)} %v_hbm.1, f32[3,3,8192]{2,1,0:T(4,128)} %feat_hbm.1, bf16[512,128]{1,0:T(8,128)(2,1)} %long_hbm.1, f32[1,8192]{1,0:T(1,128)} %bitcast.1), custom_call_target="tpu_custom_call" | custom-call | tf_op jit(solution)/shard_map/pallas_call | solution.py:348
  28.8 1.4 %shard_map.65 = bf16[128,8192]{1,0:T(8,128)(2,1)} custom-call(bf16[128,8192]{1,0:T(8,128)(2,1)S(1)} %shard_map.64.mixed), custom_call_target="tpu_custom_call" | custom-call | tf_op jit(solution)/shard_map/pallas_call | solution.py:371
